TPU v7x, 256 devices: a whole 4x4x8 slice. The times are simulated.
256 devices in a mesh: inner: 16 (over x, y), outer: 16 (over z, core).
Axes of the slice: x: 4, y: 4, z: 8, core: 2. Of those that a mesh axis runs over, the one named last changes fastest.
Arguments:
- jac: float32 [4096, 256, 256], P(('outer', 'inner')), may hold values from -0.5 to 1
- obs: float32 [4096, 256], P(('outer', 'inner')), may hold values from -6 to 6
- gain_filter: float32 [256], replicated, may hold values from 0 to 0.1
- gain_smooth: float32 [256, 256], replicated, may hold values from -0.5 to 1
- init_mean: float32 [256], replicated, may hold values from -6 to 6
Outputs:
- filtered: float32 [4096, 256], P(('outer', 'inner'))
- smoothed: float32 [4096, 256], P(('outer', 'inner'))
All inputs are finite; a program needn't handle non-finite values.
Results may differ from a plain program's by a relative error of at most 0.0003.
Values sent between devices are 32-bit elements; how exact they have to be, the bound alone decides.
No kernel may reach another device: no remote copies, remote signals or barrier semaphores. Data moves between devices by JAX's collectives and lax.ppermute only.
A program may use at most 64 MiB of HBM per device.

v0:
```python
import jax
import jax.numpy as jnp
from jax import lax
from jax.sharding import PartitionSpec as P

HIGHEST = lax.Precision.HIGHEST


def entering(part, axis, combine, identity, reverse):
    count = lax.axis_size(axis)
    place = lax.axis_index(axis)
    ahead = count - 1 - place if reverse else place
    gathered = lax.all_gather(part, axis)
    state = jnp.zeros_like(part) + jnp.asarray(identity, part.dtype)

    def one(turn, state):
        source = count - 1 - turn if reverse else turn
        return combine(state, lax.dynamic_index_in_dim(gathered, source, 0, False))

    return lax.fori_loop(0, ahead, one, state)


def last_row(state_width):
    return (jnp.arange(state_width + 1) == state_width).astype(jnp.float32)[:, None]


def identity_map(state_width):
    return jnp.concatenate(
        [jnp.eye(state_width, dtype=jnp.float32), jnp.zeros((1, state_width), jnp.float32)], 0
    )


def compose(earlier, later):
    state_width = later.shape[1]
    product = jnp.dot(earlier, later[:state_width], precision=HIGHEST)
    return product + last_row(state_width) * later[state_width][None, :]


def advance(packed, state):
    state_width = packed.shape[1]
    return jnp.dot(state, packed[:state_width], precision=HIGHEST) + packed[state_width]


def raise_power(factor, count):
    result = jnp.eye(factor.shape[0], dtype=jnp.float32)
    square = factor
    while count > 0:
        if count % 2 == 1:
            result = jnp.dot(result, square, precision=HIGHEST)
        count = count // 2
        if count > 0:
            square = jnp.dot(square, square, precision=HIGHEST)
    return result


def incoming_state(own_map, boundary, reverse):
    state_width = own_map.shape[1]
    identity = identity_map(state_width)
    inner_count = lax.axis_size("inner")
    inner_here = lax.axis_index("inner")
    gathered = lax.all_gather(own_map[None], "inner", axis=0, tiled=True)

    def absorb(running, inputs):
        before, group_total = running
        segment, position = inputs
        group_total = compose(group_total, segment)
        if reverse:
            taken = position > inner_here
        else:
            taken = position < inner_here
        before = jnp.where(taken, group_total, before)
        return ((before, group_total), None)

    (seg_before, group_total), _ = lax.scan(
        absorb,
        (identity, identity),
        (gathered, jnp.arange(inner_count, dtype=jnp.int32)),
        reverse=reverse,
    )
    group_before = entering(group_total, "outer", compose, identity, reverse)
    group_state = advance(group_before, boundary)
    return advance(seg_before, group_state)


def shards(jac, obs, gain_filter, gain_smooth, init_mean):
    state_width = jac.shape[1]
    step_count = jac.shape[0]
    retain = 1.0 - gain_filter
    bottom = last_row(state_width)

    def compose_forward(packed, inputs):
        step_matrix, measured = inputs
        moved = (
            lax.dot_general(packed, step_matrix, (((1,), (1,)), ((), ())), precision=HIGHEST)
            * retain[None, :]
        )
        return (moved + bottom * (gain_filter * measured)[None, :], None)

    forward_map, _ = lax.scan(compose_forward, identity_map(state_width), (jac, obs))
    start_state = incoming_state(forward_map, init_mean, False)

    def forward(state, inputs):
        step_matrix, measured = inputs
        predicted = jnp.dot(step_matrix, state, precision=HIGHEST)
        updated = predicted + gain_filter * (measured - predicted)
        return (updated, (predicted, updated))

    _, (predicted_all, filtered_all) = lax.scan(forward, start_state, (jac, obs))
    correction = filtered_all - predicted_all

    def backward(state, term):
        renewed = jnp.dot(gain_smooth, state, precision=HIGHEST) + term
        return (renewed, renewed)

    zero_state = jnp.zeros((state_width,), jnp.float32)
    offset_sum, _ = lax.scan(backward, zero_state, correction, reverse=True)
    step_power = raise_power(gain_smooth.T, step_count)
    backward_map = jnp.concatenate([step_power, offset_sum[None]], 0)
    after_state = incoming_state(backward_map, zero_state, True)
    _, back_states = lax.scan(backward, after_state, correction, reverse=True)
    return (filtered_all, predicted_all + back_states)


def solution(mesh):
    return jax.shard_map(
        shards,
        mesh=mesh,
        in_specs=(P(("outer", "inner"), None, None), P(("outer", "inner"), None), P(), P(), P()),
        out_specs=(P(("outer", "inner"), None), P(("outer", "inner"), None)),
        check_vma=False,
    )
```

profile of v0, /device:TPU:1, one launch (start us, length us, event | category | flops | bytes accessed | tf_op | source)
XLA Modules:
  0.0 472.3 jit_solution(15027441515699616519)
XLA Ops:
  8.0 34.6 %while.112 = (s32[]{:T(128)}, f32[257,256]{1,0:T(8,128)S(1)}, f32[16,256,256]{2,1,0:T(8,128)}, f32[256]{0:T(256)S(1)}, f32[256]{0:T(256)}, /*index=5*/f32[16,256]{1,0:T(8,128)}, s32[]{:T(128)}) while((s32[]{:T(128)}, f32[257,256]{1,0:T(8,128)S(1)}, f32[16,256,256]{2,1,0:T(8,128)}, f32[256]{0:T(256)S(1)}, f32[256]{0:T(256)}, ...), condition=%wide.region_1.2_spmd.clone, body=%wide.region_0.1_spmd.clone.sunk | while | flops 202311168 | bytes 1322585 | solution.py:99
  43.5 61.1 %all-gather.13.cloned.1.call-done = f32[16,257,256]{2,1,0:T(8,128)} async-done(((f32[1,257,256]{2,1,0:T(8,128)}), f32[16,257,256]{2,1,0:T(8,128)}) %all-gather.13.cloned.1.call-update) | async-done | bytes 4210704 | tf_op jit(solution)/shard_map/all_gather | solution.py:61
  104.6 55.9 %while.106 = (s32[]{:T(128)}, f32[257,256]{1,0:T(8,128)S(1)}, f32[257,256]{1,0:T(8,128)S(1)}, s32[16]{0:T(128)S(1)}, s32[]{:T(128)}, /*index=5*/f32[16,257,256]{2,1,0:T(8,128)}, s32[]{:T(128)}, s32[]{:T(128)}, s32[]{}) while((s32[]{:T(128)}, f32[257,256]{1,0:T(8,128)S(1)}, f32[257,256]{1,0:T(8,128)S(1)}, s32[16]{0:T(128)S(1)}, s32[]{:T(128)}, ...), condition=%wide.region_3.4_spmd, body=%wide.region_2.3_spmd.sunk | while | flops 202310912 | bytes 1846927 | solution.py:74
  106.6 1.5 broadcast_select_fusion.6
  117.1 1.5 broadcast_select_fusion.6
  127.6 1.5 broadcast_select_fusion.6
  131.1 1.5 broadcast_select_fusion.6
  134.6 1.5 broadcast_select_fusion.6
  141.5 1.5 broadcast_select_fusion.6
  152.0 1.5 broadcast_select_fusion.6
  155.5 1.5 broadcast_select_fusion.6
  163.4 40.4 %all-gather.15.cloned.1.call-done = f32[16,257,256]{2,1,0:T(8,128)} async-done(((f32[1,257,256]{2,1,0:T(8,128)}), f32[16,257,256]{2,1,0:T(8,128)}) %all-gather.15.cloned.1.call-update) | async-done | bytes 4210704 | tf_op jit(solution)/shard_map/all_gather | solution.py:13
  203.8 2.1 while.107
  206.5 33.3 %while.108 = (s32[]{:T(128)}, f32[256]{0:T(256)S(1)}, f32[16,256]{1,0:T(8,128)S(1)}, f32[16,256]{1,0:T(8,128)S(1)}, f32[16,256,256]{2,1,0:T(8,128)}, /*index=5*/...) while((s32[]{:T(128)}, f32[256]{0:T(256)S(1)}, f32[16,256]{1,0:T(8,128)S(1)}, ...), condition=%wide.region_7.8_spmd, body=%wide.region_6.7_spmd.sunk | while | flops 787202 | bytes 275049 | solution.py:108
  239.8 6.1 %while.113 = (s32[]{:T(128)}, f32[256]{0:T(256)S(1)}, f32[256,256]{1,0:T(8,128)S(1)}, f32[16,256]{1,0:T(8,128)S(1)}, s32[]{:T(128)}, /*index=5*/s32[]{:T(128)}, s32[]{:T(128)}) while((s32[]{:T(128)}, f32[256]{0:T(256)S(1)}, f32[256,256]{1,0:T(8,128)S(1)}, f32[16,256]{1,0:T(8,128)S(1)}, s32[]{:T(128)}, /*index=5*/s32[]{:T(128)}, ...), condition=%wide.region_9.10_spmd.clone, body=%wide.region_8.9_spmd.clone.sunk | while | flops 786948 | bytes 271463 | solution.py:116
  246.8 84.0 %all-gather.17.cloned.1.call-done = f32[16,257,256]{2,1,0:T(8,128)} async-done(((f32[1,257,256]{2,1,0:T(8,128)}), f32[16,257,256]{2,1,0:T(8,128)}) %all-gather.17.cloned.1.call-update) | async-done | bytes 4210704 | tf_op jit(solution)/shard_map/all_gather | solution.py:61
  330.8 54.4 %while.109 = (s32[]{:T(128)}, f32[257,256]{1,0:T(8,128)S(1)}, f32[257,256]{1,0:T(8,128)S(1)}, s32[16]{0:T(128)S(1)}, s32[]{:T(128)}, /*index=5*/f32[16,257,256]{2,1,0:T(8,128)}, s32[]{:T(128)}, s32[]{:T(128)}, s32[]{:T(128)}, s32[]{}) while((s32[]{:T(128)}, f32[257,256]{1,0:T(8,128)S(1)}, f32[257,256]{1,0:T(8,128)S(1)}, s32[16]{0:T(128)S(1)}, ...), condition=%wide.region_11.12_spmd, body=%wide.region_10.11_spmd.sunk | while | flops 202310912 | bytes 1846439 | solution.py:74
  332.7 1.5 broadcast_select_fusion.7
  346.3 1.5 broadcast_select_fusion.7
  349.7 1.5 broadcast_select_fusion.7
  370.1 1.5 broadcast_select_fusion.7
  386.0 42.6 %all-gather.19.cloned.1.call-done = f32[16,257,256]{2,1,0:T(8,128)} async-done(((f32[1,257,256]{2,1,0:T(8,128)}), f32[16,257,256]{2,1,0:T(8,128)}) %all-gather.19.cloned.1.call-update) | async-done | bytes 4210704 | tf_op jit(solution)/shard_map/all_gather | solution.py:13
  428.6 29.7 %while.110 = (s32[]{:T(128)}, f32[257,256]{1,0:T(8,128)S(1)}, s32[]{:T(128)}, f32[16,257,256]{2,1,0:T(8,128)}, s32[]{:T(128)}, /*index=5*/s32[]{:T(128)}, s32[]{:T(128)}, s32[]{:T(128)}, s32[]{}) while((s32[]{:T(128)}, f32[257,256]{1,0:T(8,128)S(1)}, s32[]{:T(128)}, f32[16,257,256]{2,1,0:T(8,128)}, s32[]{:T(128)}, /*index=5*/s32[]{:T(128)}, ...), condition=%wide.region_13.14_spmd, body=%wide.region_12.13_spmd.sunk | while | flops 202245120 | bytes 1320107 | solution.py:20
  458.8 6.3 %while.111 = (s32[]{:T(128)}, f32[256]{0:T(256)S(1)}, f32[16,256]{1,0:T(8,128)S(1)}, f32[256,256]{1,0:T(8,128)S(1)}, f32[16,256]{1,0:T(8,128)S(1)}, /*index=5*/s32[]{:T(128)}, s32[]{:T(128)}, s32[]{:T(128)}) while((s32[]{:T(128)}, f32[256]{0:T(256)S(1)}, f32[16,256]{1,0:T(8,128)S(1)}, f32[256,256]{1,0:T(8,128)S(1)}, ...), condition=%wide.region_15.16_spmd, body=%wide.region_14.15_spmd.sunk | while | flops 786691 | bytes 271465 | solution.py:120
  (537 shorter events, 188.8 us)
Async XLA Ops:
  7.2 198.8 %copy-start = (f32[256]{0:T(256)S(1)}, f32[256]{0:T(256)}, u32[]{:S(2)}) copy-start(f32[256]{0:T(256)} %param.25) | copy-start | bytes 3076
  7.2 97.4 %all-gather.13.cloned.1.call-start = ((), (), s32[]{:S(2)}) async-start(), calls=%async_computation | async-start | bytes 4595712 | tf_op jit(solution)/shard_map/all_gather | solution.py:61
  42.6 0.7 copy-start.4
  43.4 160.5 %all-gather.15.cloned.1.call-start = ((), (), s32[]{:S(2)}) async-start(), calls=%async_computation.1 | async-start | bytes 4595712 | tf_op jit(solution)/shard_map/all_gather | solution.py:13
  104.6 56.7 %copy-start.1 = (f32[256,256]{1,0:T(8,128)S(1)}, f32[256,256]{1,0:T(8,128)}, u32[]{:S(2)}) copy-start(f32[256,256]{1,0:T(8,128)} %param.24) | copy-start | bytes 786436
  160.5 0.7 copy-start.2
  161.3 169.6 %all-gather.17.cloned.1.call-start = ((), (), s32[]{:S(2)}) async-start(), calls=%async_computation.2 | async-start | bytes 4595712 | tf_op jit(solution)/shard_map/all_gather | solution.py:61
  162.7 43.8 %copy-start.5 = (f32[256]{0:T(256)S(1)}, f32[256]{0:T(256)}, u32[]{:S(2)}) copy-start(f32[256]{0:T(256)} %get-tuple-element.1116) | copy-start | bytes 3076
  239.8 91.0 %copy-start.6 = (f32[16,256]{1,0:T(8,128)}, f32[16,256]{1,0:T(8,128)S(1)}, u32[]{:S(2)}) copy-start(f32[16,256]{1,0:T(8,128)S(1)} %get-tuple-element.497) | copy-start | bytes 49156
  246.7 181.9 %all-gather.19.cloned.1.call-start = ((), (), s32[]{:S(2)}) async-start(), calls=%async_computation.3 | async-start | bytes 4595712 | tf_op jit(solution)/shard_map/all_gather | solution.py:13
  385.3 0.7 copy-start.3
Sparse Core Ops, SparseCore 0:
  43.5 61.0 all-gather.12
  161.4 42.4 all-gather.14
  246.8 83.9 all-gather.16
  386.1 42.4 all-gather.18
where the time goes:
time: 479 us; the launch traced here: 472 us
  waiting for transfers between devices  228 us (48%)
  matrix products  121 us (25%)
  local copies, waits for them, and re-layouts  70.9 us (15%)
  loops' own time  23.3 us (5%)
  other arithmetic  14.7 us (3%)
  between operations  14.1 us (3%)
    all_gather x2, waiting for transfers between devices, incoming_state(): gathered = lax.all_gather(own_map[None], 'inner', axis=0, tiled=True)  145 us
    all_gather x2, waiting for transfers between devices, entering(): gathered = lax.all_gather(part, axis)  83 us
    dot_general x47, matrix products, compose(): product = jnp.dot(earlier, later[:state_width], precision=HIGHEST)  68 us
    slice x47, local copies, waits for them, and re-layouts, compose(): return product + last_row(state_width) * later[state_width][None, :]  33.1 us
    dot_general x16, matrix products, compose_forward(): lax.dot_general(packed, step_matrix, (((1,), (1,)), ((), ())), precision=...  21.9 us
    another operation x2, loops' own time, incoming_state(): lax.scan(absorb, (identity, identity), (gathered, jnp.arange(inner_count,...  20.8 us
    dot_general x16, matrix products, forward(): predicted = jnp.dot(step_matrix, state, precision=HIGHEST)  19.6 us
    dynamic_slice x32, local copies, waits for them, and re-layouts, incoming_state(): lax.scan(absorb, (identity, identity), (gathered, jnp.arange(inner_count,...  18.6 us
  transfers between devices with their start and end apart: 4, of which 4 were waited for; matrix products, arithmetic and copies ran while one was open for 0% of the time, Pallas kernels for 0%

commit v1 on v0

v1 whole, which is shorter than its diff:
```python
import functools

import jax
import jax.numpy as jnp
from jax import lax
from jax.experimental import pallas as pl
from jax.experimental.pallas import tpu as pltpu
from jax.sharding import PartitionSpec as P

HIGHEST = lax.Precision.HIGHEST
F32 = jnp.float32
VMEM = pl.BlockSpec(memory_space=pltpu.VMEM)
SMEM = pl.BlockSpec(memory_space=pltpu.SMEM)
ANY = pl.BlockSpec(memory_space=pl.ANY)
PAD = 8


def dot_nn(a, b):
    return lax.dot_general(
        a, b, (((1,), (0,)), ((), ())), precision=HIGHEST, preferred_element_type=F32
    )


def dot_nt(a, b):
    return lax.dot_general(
        a, b, (((1,), (1,)), ((), ())), precision=HIGHEST, preferred_element_type=F32
    )


def kernel_call(body, out_shape, in_specs, args, name, scratch=(), flops=0, size=0):
    many = isinstance(out_shape, list)
    shapes = [jax.ShapeDtypeStruct(s, F32) for s in (out_shape if many else [out_shape])]
    out = pl.pallas_call(
        body,
        out_shape=shapes,
        in_specs=in_specs,
        out_specs=[VMEM] * len(shapes),
        scratch_shapes=list(scratch),
        cost_estimate=pl.CostEstimate(flops=flops, bytes_accessed=size, transcendentals=0),
        compiler_params=pltpu.CompilerParams(vmem_limit_bytes=40 << 20),
        name=name,
    )(*args)
    return out if many else out[0]


def local_map_body(jac_hbm, obs, gain, out, buf, chain, sems):
    steps, n, _ = buf.shape
    lanes = 4
    depth = steps // lanes
    order = [c * depth + i for i in range(depth) for c in range(lanes)]
    for t in order:
        pltpu.make_async_copy(jac_hbm.at[t], buf.at[t], sems.at[t]).start()
    g = gain[...]
    retain = 1.0 - g
    for i in range(depth):
        for c in range(lanes):
            t = c * depth + i
            pltpu.make_async_copy(jac_hbm.at[t], buf.at[t], sems.at[t]).wait()
            offset = jnp.broadcast_to(g * obs[t : t + 1, :], (PAD, n))
            if i == 0:
                chain[c, :n] = buf[t].T * retain
                chain[c, n:] = offset
            else:
                moved = dot_nt(chain[c], buf[t]) * retain
                chain[c, :n] = moved[:n]
                chain[c, n:] = moved[n:] + offset
    width = 1
    while width < lanes:
        for c in range(0, lanes, 2 * width):
            moved = dot_nn(chain[c], chain[c + width, :n])
            dest = out if 2 * width == lanes else chain.at[c]
            later = chain[c + width, n:]
            dest[:n] = moved[:n]
            dest[n:] = moved[n:] + later
        width *= 2


def local_map(jac, obs, gain):
    steps, n, _ = jac.shape
    return kernel_call(
        local_map_body,
        (n + PAD, n),
        [ANY, VMEM, VMEM],
        (jac, obs, gain),
        "local_map",
        scratch=[
            pltpu.VMEM((steps, n, n), F32),
            pltpu.VMEM((4, n + PAD, n), F32),
            pltpu.SemaphoreType.DMA((steps,)),
        ],
        flops=12 * steps * n**3,
        size=4 * steps * n * n,
    )


def join(earlier, later, out):
    n = out.shape[1]
    moved = dot_nn(earlier[...], later[:n])
    out[:n] = moved[:n]
    out[n:] = moved[n:] + later[n:]


def total_body(upper, own, other, out):
    @pl.when(upper[0] == 1)
    def _():
        join(other, own, out)

    @pl.when(upper[0] == 0)
    def _():
        join(own, other, out)


def before_body(upper, before, other, out):
    @pl.when(upper[0] == 1)
    def _():
        join(other, before, out)

    @pl.when(upper[0] == 0)
    def _():
        out[...] = before[...]


def pair_call(body, upper, a, b, name):
    n = a.shape[1]
    return kernel_call(
        body, a.shape, [SMEM, VMEM, VMEM], (upper, a, b), name, flops=12 * n**3, size=12 * n * n
    )


def hop_body(take, x, received, group_map, x_out, y_out):
    n = x.shape[1]
    taken = jnp.where(take[0] == 1, received[...], x[...])
    x_out[...] = taken
    y_out[...] = dot_nn(taken, group_map[:n]) + group_map[n:]


def hop(take, x, received, group_map):
    n = x.shape[1]
    return kernel_call(
        hop_body,
        [(PAD, n), (PAD, n)],
        [SMEM, VMEM, VMEM, VMEM],
        (take, x, received, group_map),
        "hop",
        flops=96 * n * n,
        size=4 * n * n,
    )


def scan_body(take, x, received, before, jac_hbm, obs, gain, smooth, pred, filt, out, buf, sems):
    steps, n, _ = buf.shape
    for t in range(steps):
        pltpu.make_async_copy(jac_hbm.at[t], buf.at[t], sems.at[t]).start()
    g = gain[...]
    state = jnp.where(take[0] == 1, received[...], x[...])
    state = dot_nn(state, before[:n]) + before[n:]
    for t in range(steps):
        pltpu.make_async_copy(jac_hbm.at[t], buf.at[t], sems.at[t]).wait()
        predicted = dot_nt(state, buf[t])
        state = predicted + g * (obs[t : t + 1, :] - predicted)
        pred[t : t + 1, :] = predicted[:1]
        filt[t : t + 1, :] = state[:1]
    back = jnp.zeros_like(state)
    gs = smooth[...]
    for t in reversed(range(steps)):
        back = dot_nt(back, gs) + (filt[t : t + 1, :] - pred[t : t + 1, :])
    out[...] = back


def forward_scan(take, x, received, before, jac, obs, gain, smooth):
    steps, n, _ = jac.shape
    return kernel_call(
        scan_body,
        [(steps, n), (steps, n), (PAD, n)],
        [SMEM, VMEM, VMEM, VMEM, ANY, VMEM, VMEM, VMEM],
        (take, x, received, before, jac, obs, gain, smooth),
        "forward_scan",
        scratch=[pltpu.VMEM((steps, n, n), F32), pltpu.SemaphoreType.DMA((steps,))],
        flops=200 * steps * n * n,
        size=4 * steps * n * n,
    )


def powers_body(steps, count, outer_count, smooth, inner, outer):
    n = smooth.shape[0]
    square = smooth[...].T
    reach = 1
    while reach < steps:
        square = dot_nn(square, square)
        reach *= 2
    for dest, number in ((inner, count), (outer, outer_count)):
        level = 0
        reach = 1
        while reach < number:
            dest[level] = square
            square = dot_nn(square, square)
            reach *= 2
            level += 1


def powers(smooth, steps, count, outer_count):
    n = smooth.shape[0]
    shapes = [(count.bit_length() - 1, n, n), (outer_count.bit_length() - 1, n, n)]
    return kernel_call(
        functools.partial(powers_body, steps, count, outer_count),
        shapes,
        [VMEM],
        (smooth,),
        "powers",
        flops=150 * n**3,
        size=40 * n * n,
    )


def lift_body(place, powers_ref, out):
    levels, n, _ = powers_ref.shape
    left = (1 << levels) - 1 - place[0]
    row = lax.broadcasted_iota(jnp.int32, (n, n), 0)
    column = lax.broadcasted_iota(jnp.int32, (n, n), 1)
    out[...] = jnp.where(row == column, 1.0, 0.0).astype(F32)
    for level in range(levels):
        @pl.when((left >> level) % 2 == 1)
        def _():
            out[...] = dot_nn(out[...], powers_ref[level])


def lift(place, powers_ref):
    levels, n, _ = powers_ref.shape
    return kernel_call(
        lift_body, (n, n), [SMEM, VMEM], (place, powers_ref), "lift", flops=48 * n**3, size=20 * n * n
    )


def fold(rows, powers_ref):
    level = 0
    while len(rows) > 1:
        half = len(rows) // 2
        later = jnp.concatenate([rows[2 * i + 1] for i in range(half)], 0)
        moved = dot_nn(later, powers_ref[level])
        rows = [rows[2 * i] + moved[PAD * i : PAD * (i + 1)] for i in range(half)]
        level += 1
    return rows[0]


def gather_fold(place, got, powers_ref):
    count, n = got.shape
    sub = lax.broadcasted_iota(jnp.int32, (PAD, n), 0)
    rows = []
    for k in range(count):
        source = place[0] + 1 + k
        inside = source < count
        mine = got[pl.ds(jnp.where(inside, source, 0), 1), :]
        mine = jnp.where(inside, mine, jnp.zeros_like(mine))
        rows.append(
            jnp.where(
                sub < 4, jnp.broadcast_to(mine, (PAD, n)), jnp.broadcast_to(got[k : k + 1, :], (PAD, n))
            )
        )
    return fold(rows, powers_ref)


def inner_body(place, got, powers_ref, after, total):
    both = gather_fold(place, got, powers_ref)
    n = both.shape[1]
    after[...] = jnp.broadcast_to(both[:1], (PAD, n))
    total[...] = jnp.broadcast_to(both[4:5], total.shape)


def backward_body(place, got, powers_ref, after, lifted, pred, filt, smooth, out):
    both = gather_fold(place, got, powers_ref)
    steps, n = pred.shape
    boundary = jnp.broadcast_to(both[:1], (PAD, n))
    back = after[...] + dot_nn(boundary, lifted[...])
    gs = smooth[...]
    for t in reversed(range(steps)):
        back = dot_nt(back, gs) + (filt[t : t + 1, :] - pred[t : t + 1, :])
        out[t : t + 1, :] = pred[t : t + 1, :] + back[:1]


def shards(jac, obs, gain_filter, gain_smooth, init_mean):
    steps, n, _ = jac.shape
    inner_count, outer_count = lax.axis_size("inner"), lax.axis_size("outer")
    inner, outer = lax.axis_index("inner"), lax.axis_index("outer")
    gain = gain_filter[None, :]

    def bit(index, k):
        return ((index >> k) % 2).astype(jnp.int32)[None]

    with jax.named_scope("compose"):
        total = local_map(jac, obs, gain)
    before = None
    stages = [("inner", inner, 1, 0), ("inner", inner, 3, 1), ("inner", inner, 4, 2), ("inner", inner, 12, 3)]
    stages += [("outer", outer, 1, 0), ("outer", outer, 2, 1)]
    counts = {"inner": inner_count, "outer": outer_count}
    for axis, index, flip, k in stages:
        with jax.named_scope(f"join_{axis}_{k}"):
            other = lax.ppermute(total, axis, [(i, i ^ flip) for i in range(counts[axis])])
            upper = bit(index, k)
            if before is None:
                eye = jnp.concatenate([jnp.eye(n, dtype=F32), jnp.zeros((PAD, n), F32)], 0)
                before = jnp.where(upper[0] == 1, other, eye)
            else:
                before = pair_call(before_body, upper, before, other, "before")
            total = pair_call(total_body, upper, total, other, "total")
    inner_powers, outer_powers = powers(gain_smooth, steps, inner_count, outer_count)
    place = inner.astype(jnp.int32)[None]
    lifted = lift(place, inner_powers)

    x = jnp.broadcast_to(init_mean[None, :], (PAD, n))
    received = x
    group = 4
    supers = outer_count // group
    chain = [(i, i + group) for i in range(outer_count - group)]
    for h in range(supers - 1):
        with jax.named_scope(f"hop_{h}"):
            take = (outer // group == h).astype(jnp.int32)[None]
            x, y = hop(take, x, received, total)
            received = lax.ppermute(y, "outer", chain)
    take = (outer // group == supers - 1).astype(jnp.int32)[None]
    with jax.named_scope("forward"):
        pred, filt, offset = forward_scan(take, x, received, before, jac, obs, gain, gain_smooth)
    with jax.named_scope("suffix_inner"):
        sent = jnp.broadcast_to(offset[:1], (inner_count, n))
        got = lax.all_to_all(sent, "inner", 0, 0, tiled=True)
        after, group_total = kernel_call(
            inner_body,
            [(PAD, n), (outer_count, n)],
            [SMEM, VMEM, VMEM],
            (place, got, inner_powers),
            "suffix_inner",
            flops=100 * n * n,
            size=16 * n * n,
        )
    with jax.named_scope("suffix_outer"):
        got = lax.all_to_all(group_total, "outer", 0, 0, tiled=True)
        smoothed = kernel_call(
            backward_body,
            (steps, n),
            [SMEM] + [VMEM] * 7,
            (outer.astype(jnp.int32)[None], got, outer_powers, after, lifted, pred, filt, gain_smooth),
            "backward",
            flops=200 * n * n,
            size=24 * n * n,
        )
    return (filt, smoothed)


def solution(mesh):
    return jax.shard_map(
        shards,
        mesh=mesh,
        in_specs=(P(("outer", "inner"), None, None), P(("outer", "inner"), None), P(), P(), P()),
        out_specs=(P(("outer", "inner"), None), P(("outer", "inner"), None)),
        check_vma=False,
    )
```

time: 479 us -> 141 us (0.29); the launches traced: 472 us -> 140 us
  waiting for transfers between devices: 228 us -> 34 us
  matrix products: 121 us -> 0 us
  local copies, waits for them, and re-layouts: 70.9 us -> 4.88 us
  starting transfers between devices: 0.16 us -> 54.3 us
  Pallas kernels: 0 us -> 46.3 us
  loops' own time: 23.3 us -> 0 us
  other arithmetic: 14.7 us -> 0.05 us
  between operations: 14.1 us -> 0.88 us
    all_gather x4 -> x0, waiting for transfers between devices: 228 us -> none  [the longest x2 145 us: incoming_state(): gathered = lax.all_gather(own_map[None], 'inner', axis=0, tiled=True)]
    dot_general x120 -> x0, matrix products: 121 us -> none  [the longest x47 68 us: compose(): product = jnp.dot(earlier, later[:state_width], precision=HIGHEST)]
    pallas_call x0 -> x20, Pallas kernels: none -> 46.3 us  [kernel_call(): pl.pallas_call(body, out_shape=shapes, in_specs=in_specs, out_specs=[VMEM...]
    slice x51 -> x1, local copies, waits for them, and re-layouts: 33.1 us -> 0.01 us  [shards(): sent = jnp.broadcast_to(offset[:1], (inner_count, n))]
    ppermute x0 -> x9, starting transfers between devices: none -> 33.1 us  [the longest x6 16.7 us: shards(): lax.ppermute(total, axis, [(i, i ^ flip) for i in range(counts[axis])])]
    dynamic_slice x80 -> x0, local copies, waits for them, and re-layouts: 31.8 us -> none  [the longest x32 18.6 us: incoming_state(): lax.scan(absorb, (identity, identity), (gathered, jnp.arange(inner_count,...]
    ppermute x0 -> x9, waiting for transfers between devices: none -> 27.5 us  [the longest x6 25.6 us: shards(): lax.ppermute(total, axis, [(i, i ^ flip) for i in range(counts[axis])])]
    another operation x8 -> x0, loops' own time: 23.3 us -> none  [the longest x2 20.8 us: incoming_state(): lax.scan(absorb, (identity, identity), (gathered, jnp.arange(inner_count,...]
  transfers between devices with their start and end apart: 4 -> 11, of which waited for: 4 -> 11; matrix products, arithmetic and copies ran while one was open for 0% -> 0% of each run, Pallas kernels for 0% -> 6%
where the time goes in v1:
time: 141 us; the launch traced here: 140 us
  starting transfers between devices  54.3 us (39%)
  Pallas kernels  46.3 us (33%)
  waiting for transfers between devices  34 us (24%)
  local copies, waits for them, and re-layouts  4.88 us (3%)
    pallas_call x20, Pallas kernels, kernel_call(): pl.pallas_call(body, out_shape=shapes, in_specs=in_specs, out_specs=[VMEM...  46.3 us
    ppermute x6, waiting for transfers between devices, shards(): lax.ppermute(total, axis, [(i, i ^ flip) for i in range(counts[axis])])  25.6 us
    ppermute x6, starting transfers between devices, shards(): lax.ppermute(total, axis, [(i, i ^ flip) for i in range(counts[axis])])  16.7 us
    ppermute x3, starting transfers between devices, shards(): received = lax.ppermute(y, 'outer', chain)  16.4 us
    all_to_all x1, starting transfers between devices, shards(): got = lax.all_to_all(group_total, 'outer', 0, 0, tiled=True)  14.9 us
    all_to_all x1, starting transfers between devices, shards(): got = lax.all_to_all(sent, 'inner', 0, 0, tiled=True)  6.25 us
    all_to_all x1, waiting for transfers between devices, shards(): got = lax.all_to_all(group_total, 'outer', 0, 0, tiled=True)  5.78 us
    unnamed x20, local copies, waits for them, and re-layouts  3.62 us
  transfers between devices with their start and end apart: 11, of which 11 were waited for; matrix products, arithmetic and copies ran while one was open for 0% of the time, Pallas kernels for 6%

profile of v1, /device:TPU:1, one launch (start us, length us, event | category | flops | bytes accessed | tf_op | source)
XLA Modules:
  0.0 140.4 jit_solution(13563561926293806776)
XLA Ops:
  0.6 2.2 %copy-done = f32[16,256,256]{2,1,0:T(8,128)S(1)} copy-done((f32[16,256,256]{2,1,0:T(8,128)S(1)}, f32[16,256,256]{2,1,0:T(8,128)}, u32[]{:S(2)}) %copy-start) | copy-done | bytes 4194328
  4.2 9.1 %local_map.1.own = f32[264,256]{1,0:T(8,128)S(1)} custom-call(f32[16,256,256]{2,1,0:T(8,128)S(1)} %copy-done, f32[16,256]{1,0:T(8,128)S(1)} %copy-done.3, f32[1,256]{1,0:T(1,128)S(1)} %bitcast.24), custom_call_target="tpu_custom_call" | custom-call | flops 3221225472 | bytes 4194304 | tf_op jit(solution)/shard_map/compose/local_map/pallas_call | solution.py:33
  13.4 2.2 %collective-permute-start = (f32[264,256]{1,0:T(8,128)S(1)}, f32[264,256]{1,0:T(8,128)S(1)}, u32[]{:S(2)}, u32[]{:S(2)}) collective-permute-start(f32[264,256]{1,0:T(8,128)S(1)} %local_map.1.own), channel_id=1, source_target_pairs={{0,16},{16,0},{32,48},{48,32},{64,80},{80,64},{96,112},{112,96},{1... | collective-permute-start | bytes 811016 | tf_op jit(solution)/shard_map/join_inner_0/ppermute | solution.py:297
  15.6 5.0 %collective-permute-done.other = f32[264,256]{1,0:T(8,128)S(1)} collective-permute-done((f32[264,256]{1,0:T(8,128)S(1)}, f32[264,256]{1,0:T(8,128)S(1)}, u32[]{:S(2)}, u32[]{:S(2)}) %collective-permute-start) | collective-permute-done | bytes 270368 | tf_op jit(solution)/shard_map/join_inner_0/ppermute | solution.py:297
  20.9 3.9 %collective-permute-start.1 = (f32[264,256]{1,0:T(8,128)S(1)}, f32[264,256]{1,0:T(8,128)S(1)}, u32[]{:S(2)}, u32[]{:S(2)}) collective-permute-start(f32[264,256]{1,0:T(8,128)S(1)} %total.6.own), channel_id=1, source_target_pairs={{0,48},{16,32},{32,16},{48,0},{64,112},{80,96},{96,80},{112,64},{1... | collective-permute-start | bytes 811016 | tf_op jit(solution)/shard_map/join_inner_1/ppermute | solution.py:297
  24.9 5.1 %collective-permute-done.1.other = f32[264,256]{1,0:T(8,128)S(1)} collective-permute-done((f32[264,256]{1,0:T(8,128)S(1)}, f32[264,256]{1,0:T(8,128)S(1)}, u32[]{:S(2)}, u32[]{:S(2)}) %collective-permute-start.1) | collective-permute-done | bytes 270368 | tf_op jit(solution)/shard_map/join_inner_1/ppermute | solution.py:297
  30.3 1.3 collective-permute-start.2
  31.6 4.1 %collective-permute-done.2.other = f32[264,256]{1,0:T(8,128)S(1)} collective-permute-done((f32[264,256]{1,0:T(8,128)S(1)}, f32[264,256]{1,0:T(8,128)S(1)}, u32[]{:S(2)}, u32[]{:S(2)}) %collective-permute-start.2) | collective-permute-done | bytes 270368 | tf_op jit(solution)/shard_map/join_inner_2/ppermute | solution.py:297
  36.1 2.6 %collective-permute-start.3 = (f32[264,256]{1,0:T(8,128)S(1)}, f32[264,256]{1,0:T(8,128)S(1)}, u32[]{:S(2)}, u32[]{:S(2)}) collective-permute-start(f32[264,256]{1,0:T(8,128)S(1)} %total.8.own), channel_id=1, source_target_pairs={{0,192},{16,208},{32,224},{48,240},{64,128},{80,144},{96,160},{112... | collective-permute-start | bytes 811016 | tf_op jit(solution)/shard_map/join_inner_3/ppermute | solution.py:297
  38.7 4.1 %collective-permute-done.3.other = f32[264,256]{1,0:T(8,128)S(1)} collective-permute-done((f32[264,256]{1,0:T(8,128)S(1)}, f32[264,256]{1,0:T(8,128)S(1)}, u32[]{:S(2)}, u32[]{:S(2)}) %collective-permute-start.3) | collective-permute-done | bytes 270368 | tf_op jit(solution)/shard_map/join_inner_3/ppermute | solution.py:297
  43.1 5.0 %collective-permute-start.4 = (f32[264,256]{1,0:T(8,128)S(1)}, f32[264,256]{1,0:T(8,128)S(1)}, u32[]{:S(2)}, u32[]{:S(2)}) collective-permute-start(f32[264,256]{1,0:T(8,128)S(1)} %total.9.own), channel_id=1, source_target_pairs={{0,1},{1,0},{2,3},{3,2},{4,5},{5,4},{6,7},{7,6},{8,9},{9,8},{10,11... | collective-permute-start | bytes 811016 | tf_op jit(solution)/shard_map/join_outer_0/ppermute | solution.py:297
  48.2 1.1 collective-permute-done.4.other
  49.7 1.7 %collective-permute-start.5 = (f32[264,256]{1,0:T(8,128)S(1)}, f32[264,256]{1,0:T(8,128)S(1)}, u32[]{:S(2)}, u32[]{:S(2)}) collective-permute-start(f32[264,256]{1,0:T(8,128)S(1)} %total.10.own), channel_id=1, source_target_pairs={{0,2},{1,3},{2,0},{3,1},{4,6},{5,7},{6,4},{7,5},{8,10},{9,11},{10,... | collective-permute-start | bytes 811016 | tf_op jit(solution)/shard_map/join_outer_1/ppermute | solution.py:297
  51.5 6.3 %collective-permute-done.5.other = f32[264,256]{1,0:T(8,128)S(1)} collective-permute-done((f32[264,256]{1,0:T(8,128)S(1)}, f32[264,256]{1,0:T(8,128)S(1)}, u32[]{:S(2)}, u32[]{:S(2)}) %collective-permute-start.5) | collective-permute-done | bytes 270368 | tf_op jit(solution)/shard_map/join_outer_1/ppermute | solution.py:297
  58.4 4.9 %collective-permute-start.6 = (f32[8,256]{1,0:T(8,128)S(1)}, f32[8,256]{1,0:T(8,128)S(1)}, u32[]{:S(2)}, u32[]{:S(2)}) collective-permute-start(f32[8,256]{1,0:T(8,128)S(1)} %get-tuple-element.16), channel_id=1, source_target_pairs={{0,4},{1,5},{2,6},{3,7},{4,8},{5,9},{6,10},{7,11},{8,12},{9,13},{1... | collective-permute-start | bytes 24584 | tf_op jit(solution)/shard_map/hop_0/ppermute | solution.py:318
  64.3 5.7 %collective-permute-start.7 = (f32[8,256]{1,0:T(8,128)S(1)}, f32[8,256]{1,0:T(8,128)S(1)}, u32[]{:S(2)}, u32[]{:S(2)}) collective-permute-start(f32[8,256]{1,0:T(8,128)S(1)} %get-tuple-element.18), channel_id=1, source_target_pairs={{0,4},{1,5},{2,6},{3,7},{4,8},{5,9},{6,10},{7,11},{8,12},{9,13},{1... | collective-permute-start | bytes 24584 | tf_op jit(solution)/shard_map/hop_1/ppermute | solution.py:318
  71.1 5.8 %collective-permute-start.8 = (f32[8,256]{1,0:T(8,128)S(1)}, f32[8,256]{1,0:T(8,128)S(1)}, u32[]{:S(2)}, u32[]{:S(2)}) collective-permute-start(f32[8,256]{1,0:T(8,128)S(1)} %get-tuple-element.20), channel_id=1, source_target_pairs={{0,4},{1,5},{2,6},{3,7},{4,8},{5,9},{6,10},{7,11},{8,12},{9,13},{1... | collective-permute-start | bytes 24584 | tf_op jit(solution)/shard_map/hop_2/ppermute | solution.py:318
  77.7 16.0 %forward_scan.1 = (f32[16,256]{1,0:T(8,128)S(1)}, f32[16,256]{1,0:T(8,128)}, f32[8,256]{1,0:T(8,128)S(1)}) custom-call(s32[1]{0:T(128)} %bitcast.take, f32[8,256]{1,0:T(8,128)S(1)} %get-tuple-element.19.x, f32[8,256]{1,0:T(8,128)S(1)} %collective-permute-done.8.received, f32[264,256]{1,0:T(8,128)S(1)} %before.9, f32[16,256,256]{2,1,0:T(8,128)S(1)} %copy-done.1, ...), custom_call_target="tpu_custom_call" | custom-call | flops 209715200 | bytes 4194304 | tf_op jit(solution)/shard_map/forward/forward_scan/pallas_call | solution.py:33
  94.3 6.3 %all-to-all-start = ((f32[16,1,256]{2,1,0:T(1,128)}), f32[16,1,256]{2,1,0:T(1,128)S(1)}, u32[]{:S(2)}, u32[]{:S(2)}) async-start(f32[16,1,256]{2,1,0:T(1,128)} %broadcast_in_dim.77), calls=%async_computation | async-start | bytes 32768 | tf_op jit(solution)/shard_map/suffix_inner/all_to_all | solution.py:324
  100.6 5.7 %powers.1 = (f32[4,256,256]{2,1,0:T(8,128)S(1)}, f32[4,256,256]{2,1,0:T(8,128)S(1)}) custom-call(f32[256,256]{1,0:T(8,128)S(1)} %copy-done.2), custom_call_target="tpu_custom_call" | custom-call | flops 2516582400 | bytes 2621440 | tf_op jit(solution)/shard_map/powers/pallas_call | solution.py:33
  108.8 14.9 %all-to-all-start.1 = ((f32[16,1,256]{2,1,0:T(1,128)}), f32[16,1,256]{2,1,0:T(1,128)S(1)}, u32[]{:S(2)}, u32[]{:S(2)}) async-start(f32[16,1,256]{2,1,0:T(1,128)} %copy.7), calls=%async_computation.1 | async-start | bytes 32768 | tf_op jit(solution)/shard_map/suffix_outer/all_to_all | solution.py:335
  123.7 1.5 %lift.1.lifted = f32[256,256]{1,0:T(8,128)S(1)} custom-call(s32[1]{0:T(128)} %bitcast.12.place, f32[4,256,256]{2,1,0:T(8,128)S(1)} %get-tuple-element.23.powers_ref), custom_call_target="tpu_custom_call" | custom-call | flops 805306368 | bytes 1310720 | tf_op jit(solution)/shard_map/lift/pallas_call | solution.py:33
  125.3 5.8 %all-to-all-done.1 = f32[16,1,256]{2,1,0:T(1,128)S(1)} async-done(((f32[16,1,256]{2,1,0:T(1,128)}), f32[16,1,256]{2,1,0:T(1,128)S(1)}, u32[]{:S(2)}, u32[]{:S(2)}) %all-to-all-start.1) | async-done | bytes 16416 | tf_op jit(solution)/shard_map/suffix_outer/all_to_all | solution.py:335
  131.0 9.3 %backward.1 = f32[16,256]{1,0:T(8,128)} custom-call(s32[1]{0:T(128)} %bitcast.11.place, f32[16,256]{1,0:T(8,128)S(1)} %bitcast.21, f32[4,256,256]{2,1,0:T(8,128)S(1)} %get-tuple-element.25.powers_ref, f32[8,256]{1,0:T(8,128)S(1)} %get-tuple-element.26.after, f32[256,256]{1,0:T(8,128)S(1)} %lift.1.lifted, f32[16,256]{1,0:T(8,128)S(1)} %get-tuple-element.27.pred, ...), custom_call_target="tpu_custom_call" | custom-call | flops 13107200 | bytes 1572864 | tf_op jit(solution)/shard_map/suffix_outer/backward/pallas_call | solution.py:33
  (44 shorter events, 9.9 us)
Async XLA Ops:
  0.6 2.2 %copy-start = (f32[16,256,256]{2,1,0:T(8,128)S(1)}, f32[16,256,256]{2,1,0:T(8,128)}, u32[]{:S(2)}) copy-start(f32[16,256,256]{2,1,0:T(8,128)} %jac_hbm.3) | copy-start | bytes 12582916
  2.8 0.7 copy-start.3
  3.5 0.7 copy-start.6
  13.4 44.8 %copy-start.8 = (f32[256]{0:T(256)S(1)}, f32[256]{0:T(256)}, u32[]{:S(2)}) copy-start(f32[256]{0:T(256)} %param.9) | copy-start | bytes 3076
  13.4 7.2 %collective-permute-start = (f32[264,256]{1,0:T(8,128)S(1)}, f32[264,256]{1,0:T(8,128)S(1)}, u32[]{:S(2)}, u32[]{:S(2)}) collective-permute-start(f32[264,256]{1,0:T(8,128)S(1)} %local_map.1.own), channel_id=1, source_target_pairs={{0,16},{16,0},{32,48},{48,32},{64,80},{80,64},{96,112},{112,96},{1... | collective-permute-start | bytes 811016 | tf_op jit(solution)/shard_map/join_inner_0/ppermute | solution.py:297
  20.9 9.0 %collective-permute-start.1 = (f32[264,256]{1,0:T(8,128)S(1)}, f32[264,256]{1,0:T(8,128)S(1)}, u32[]{:S(2)}, u32[]{:S(2)}) collective-permute-start(f32[264,256]{1,0:T(8,128)S(1)} %total.6.own), channel_id=1, source_target_pairs={{0,48},{16,32},{32,16},{48,0},{64,112},{80,96},{96,80},{112,64},{1... | collective-permute-start | bytes 811016 | tf_op jit(solution)/shard_map/join_inner_1/ppermute | solution.py:297
  30.3 5.4 %collective-permute-start.2 = (f32[264,256]{1,0:T(8,128)S(1)}, f32[264,256]{1,0:T(8,128)S(1)}, u32[]{:S(2)}, u32[]{:S(2)}) collective-permute-start(f32[264,256]{1,0:T(8,128)S(1)} %total.7.own), channel_id=1, source_target_pairs={{0,64},{16,80},{32,96},{48,112},{64,0},{80,16},{96,32},{112,48},{1... | collective-permute-start | bytes 811016 | tf_op jit(solution)/shard_map/join_inner_2/ppermute | solution.py:297
  36.1 41.6 %copy-start.2 = (f32[256,256]{1,0:T(8,128)S(1)}, f32[256,256]{1,0:T(8,128)}, u32[]{:S(2)}) copy-start(f32[256,256]{1,0:T(8,128)} %smooth.5) | copy-start | bytes 786436
  36.1 41.6 %copy-start.4 = (f32[16,256]{1,0:T(8,128)S(1)}, f32[16,256]{1,0:T(8,128)}, u32[]{:S(2)}) copy-start(f32[16,256]{1,0:T(8,128)} %obs.3) | copy-start | bytes 49156
  36.1 41.5 %copy-start.7 = (f32[256]{0:T(256)S(1)}, f32[256]{0:T(256)}, u32[]{:S(2)}) copy-start(f32[256]{0:T(256)} %param.7) | copy-start | bytes 3076
  36.1 6.6 %collective-permute-start.3 = (f32[264,256]{1,0:T(8,128)S(1)}, f32[264,256]{1,0:T(8,128)S(1)}, u32[]{:S(2)}, u32[]{:S(2)}) collective-permute-start(f32[264,256]{1,0:T(8,128)S(1)} %total.8.own), channel_id=1, source_target_pairs={{0,192},{16,208},{32,224},{48,240},{64,128},{80,144},{96,160},{112... | collective-permute-start | bytes 811016 | tf_op jit(solution)/shard_map/join_inner_3/ppermute | solution.py:297
  43.1 6.2 %collective-permute-start.4 = (f32[264,256]{1,0:T(8,128)S(1)}, f32[264,256]{1,0:T(8,128)S(1)}, u32[]{:S(2)}, u32[]{:S(2)}) collective-permute-start(f32[264,256]{1,0:T(8,128)S(1)} %total.9.own), channel_id=1, source_target_pairs={{0,1},{1,0},{2,3},{3,2},{4,5},{5,4},{6,7},{7,6},{8,9},{9,8},{10,11... | collective-permute-start | bytes 811016 | tf_op jit(solution)/shard_map/join_outer_0/ppermute | solution.py:297
  48.1 29.5 %copy-start.1 = (f32[16,256,256]{2,1,0:T(8,128)S(1)}, f32[16,256,256]{2,1,0:T(8,128)}, u32[]{:S(2)}) copy-start(f32[16,256,256]{2,1,0:T(8,128)} %jac_hbm.3) | copy-start | bytes 12582916
  49.7 8.1 %collective-permute-start.5 = (f32[264,256]{1,0:T(8,128)S(1)}, f32[264,256]{1,0:T(8,128)S(1)}, u32[]{:S(2)}, u32[]{:S(2)}) collective-permute-start(f32[264,256]{1,0:T(8,128)S(1)} %total.10.own), channel_id=1, source_target_pairs={{0,2},{1,3},{2,0},{3,1},{4,6},{5,7},{6,4},{7,5},{8,10},{9,11},{10,... | collective-permute-start | bytes 811016 | tf_op jit(solution)/shard_map/join_outer_1/ppermute | solution.py:297
  58.4 5.7 %collective-permute-start.6 = (f32[8,256]{1,0:T(8,128)S(1)}, f32[8,256]{1,0:T(8,128)S(1)}, u32[]{:S(2)}, u32[]{:S(2)}) collective-permute-start(f32[8,256]{1,0:T(8,128)S(1)} %get-tuple-element.16), channel_id=1, source_target_pairs={{0,4},{1,5},{2,6},{3,7},{4,8},{5,9},{6,10},{7,11},{8,12},{9,13},{1... | collective-permute-start | bytes 24584 | tf_op jit(solution)/shard_map/hop_0/ppermute | solution.py:318
  64.3 6.5 %collective-permute-start.7 = (f32[8,256]{1,0:T(8,128)S(1)}, f32[8,256]{1,0:T(8,128)S(1)}, u32[]{:S(2)}, u32[]{:S(2)}) collective-permute-start(f32[8,256]{1,0:T(8,128)S(1)} %get-tuple-element.18), channel_id=1, source_target_pairs={{0,4},{1,5},{2,6},{3,7},{4,8},{5,9},{6,10},{7,11},{8,12},{9,13},{1... | collective-permute-start | bytes 24584 | tf_op jit(solution)/shard_map/hop_1/ppermute | solution.py:318
  71.1 6.6 %collective-permute-start.8 = (f32[8,256]{1,0:T(8,128)S(1)}, f32[8,256]{1,0:T(8,128)S(1)}, u32[]{:S(2)}, u32[]{:S(2)}) collective-permute-start(f32[8,256]{1,0:T(8,128)S(1)} %get-tuple-element.20), channel_id=1, source_target_pairs={{0,4},{1,5},{2,6},{3,7},{4,8},{5,9},{6,10},{7,11},{8,12},{9,13},{1... | collective-permute-start | bytes 24584 | tf_op jit(solution)/shard_map/hop_2/ppermute | solution.py:318
  94.3 12.7 %all-to-all-start = ((f32[16,1,256]{2,1,0:T(1,128)}), f32[16,1,256]{2,1,0:T(1,128)S(1)}, u32[]{:S(2)}, u32[]{:S(2)}) async-start(f32[16,1,256]{2,1,0:T(1,128)} %broadcast_in_dim.77), calls=%async_computation | async-start | bytes 32768 | tf_op jit(solution)/shard_map/suffix_inner/all_to_all | solution.py:324
  106.3 24.8 %copy-start.5 = (f32[16,256]{1,0:T(8,128)S(1)}, f32[16,256]{1,0:T(8,128)}, u32[]{:S(2)}) copy-start(f32[16,256]{1,0:T(8,128)} %get-tuple-element.13.filt) | copy-start | bytes 49156
  108.8 22.3 %all-to-all-start.1 = ((f32[16,1,256]{2,1,0:T(1,128)}), f32[16,1,256]{2,1,0:T(1,128)S(1)}, u32[]{:S(2)}, u32[]{:S(2)}) async-start(f32[16,1,256]{2,1,0:T(1,128)} %copy.7), calls=%async_computation.1 | async-start | bytes 32768 | tf_op jit(solution)/shard_map/suffix_outer/all_to_all | solution.py:335

commit v2 on v1

v2 whole, which is shorter than its diff:
```python
import functools

import jax
import jax.numpy as jnp
from jax import lax
from jax.experimental import pallas as pl
from jax.experimental.pallas import tpu as pltpu
from jax.sharding import PartitionSpec as P

HIGHEST = lax.Precision.HIGHEST
F32 = jnp.float32
VMEM = pl.BlockSpec(memory_space=pltpu.VMEM)
SMEM = pl.BlockSpec(memory_space=pltpu.SMEM)
HBM = pl.BlockSpec(memory_space=pltpu.MemorySpace.HBM)
PAD = 8


def dot_nn(a, b):
    return lax.dot_general(
        a, b, (((1,), (0,)), ((), ())), precision=HIGHEST, preferred_element_type=F32
    )


def dot_nt(a, b):
    return lax.dot_general(
        a, b, (((1,), (1,)), ((), ())), precision=HIGHEST, preferred_element_type=F32
    )


def kernel_call(body, out_shape, in_specs, args, name, scratch=(), flops=0, size=0, grant=4):
    many = isinstance(out_shape, list)
    shapes = [jax.ShapeDtypeStruct(s, F32) for s in (out_shape if many else [out_shape])]
    out = pl.pallas_call(
        body,
        out_shape=shapes,
        in_specs=in_specs,
        out_specs=[VMEM] * len(shapes),
        scratch_shapes=list(scratch),
        cost_estimate=pl.CostEstimate(flops=flops, bytes_accessed=size, transcendentals=0),
        compiler_params=pltpu.CompilerParams(vmem_limit_bytes=grant << 20),
        name=name,
    )(*args)
    return out if many else out[0]


def local_map_body(jac_hbm, obs_hbm, gain_hbm, out, quarter, half, third, buf, obs, gain, chain, sems):
    steps, n, _ = buf.shape
    small = [(obs_hbm, obs, steps), (gain_hbm, gain, steps + 1)]
    for source, dest, k in small:
        pltpu.make_async_copy(source, dest, sems.at[k]).start()
    pairs = steps // 2
    order = [2 * c + i for i in range(2) for c in range(pairs)]
    for t in order:
        pltpu.make_async_copy(jac_hbm.at[t], buf.at[t], sems.at[t]).start()
    for source, dest, k in small:
        pltpu.make_async_copy(source, dest, sems.at[k]).wait()
    g = gain[...]
    retain = 1.0 - g
    for t in order:
        pltpu.make_async_copy(jac_hbm.at[t], buf.at[t], sems.at[t]).wait()
        c = t // 2
        offset = jnp.broadcast_to(g * obs[t : t + 1, :], (PAD, n))
        if t % 2 == 0:
            chain[c, :n] = buf[t].T * retain
            chain[c, n:] = offset
        else:
            moved = dot_nt(chain[c], buf[t]) * retain
            chain[c, :n] = moved[:n]
            chain[c, n:] = moved[n:] + offset
    kept = {(0, pairs): out, (0, pairs // 2): half}
    kept[(0, pairs // 4)] = quarter
    kept[(pairs // 2, 3 * pairs // 4)] = third
    width = 1
    while width < pairs:
        for c in range(0, pairs, 2 * width):
            moved = dot_nn(chain[c], chain[c + width, :n])
            later = chain[c + width, n:]
            span = (c, c + 2 * width)
            dest = kept.get(span, chain.at[c])
            dest[:n] = moved[:n]
            dest[n:] = moved[n:] + later
            if span in kept and 2 * width < pairs:
                chain[c] = dest[...]
        width *= 2


def local_map(jac, obs, gain):
    steps, n, _ = jac.shape
    return kernel_call(
        local_map_body,
        [(n + PAD, n)] * 4,
        [HBM, HBM, HBM],
        (jac, obs, gain),
        "local_map",
        scratch=[
            pltpu.VMEM((steps, n, n), F32),
            pltpu.VMEM((steps, n), F32),
            pltpu.VMEM((1, n), F32),
            pltpu.VMEM((steps // 2, n + PAD, n), F32),
            pltpu.SemaphoreType.DMA((steps + 2,)),
        ],
        flops=12 * steps * n**3,
        size=4 * steps * n * n,
        grant=52,
    )


def join(earlier, later, out):
    n = out.shape[1]
    moved = dot_nn(earlier[...], later[:n])
    out[:n] = moved[:n]
    out[n:] = moved[n:] + later[n:]


def total_body(upper, own, other, out):
    @pl.when(upper[0] == 1)
    def _():
        join(other, own, out)

    @pl.when(upper[0] == 0)
    def _():
        join(own, other, out)


def before_body(upper, before, other, out):
    @pl.when(upper[0] == 1)
    def _():
        join(other, before, out)

    @pl.when(upper[0] == 0)
    def _():
        out[...] = before[...]


def pair_call(body, upper, a, b, name):
    n = a.shape[1]
    return kernel_call(
        body, a.shape, [SMEM, VMEM, VMEM], (upper, a, b), name, flops=12 * n**3, size=12 * n * n
    )


def join_body(earlier, later, out):
    join(earlier, later, out)


def advance_body(count, *refs):
    x, maps, out = refs[0], refs[1 : 1 + count], refs[1 + count]
    n = x.shape[1]
    state = x[...]
    for m in maps:
        state = dot_nn(state, m[:n]) + m[n:]
    out[...] = state


def advance(x, *maps):
    n = x.shape[1]
    return kernel_call(
        functools.partial(advance_body, len(maps)),
        (PAD, n),
        [VMEM] * (1 + len(maps)),
        (x, *maps),
        "advance",
        flops=96 * n * n,
        size=4 * n * n,
    )


def forward_body(
    x, before, quarter, half, three, jac_hbm, obs, gain, base_powers, filt, base, sent, pred, shifted, jac, sems
):
    steps, n, _ = jac.shape
    lanes = 4
    depth = steps // lanes
    for i in range(depth):
        for c in range(lanes):
            t = c * depth + i
            pltpu.make_async_copy(jac_hbm.at[t], jac.at[t], sems.at[t]).start()
    g = gain[...]
    state = dot_nn(x[...], before[:n]) + before[n:]
    states = [state] + [dot_nn(state, m[:n]) + m[n:] for m in (quarter, half, three)]
    for i in range(depth):
        for c in range(lanes):
            t = c * depth + i
            pltpu.make_async_copy(jac_hbm.at[t], jac.at[t], sems.at[t]).wait()
            predicted = dot_nt(states[c], jac[t])
            states[c] = predicted + g * (obs[t : t + 1, :] - predicted)
            pred[t : t + 1, :] = predicted[:1]
            filt[t : t + 1, :] = states[c][:1]
    back = filt[...] - pred[...]
    shifted[steps:, :] = jnp.zeros((steps, n), F32)
    level = 0
    reach = 1
    while reach < steps:
        shifted[:steps, :] = back
        back = back + dot_nn(shifted[reach : reach + steps, :], base_powers[level])
        reach *= 2
        level += 1
    base[...] = pred[...] + back
    sent[...] = jnp.broadcast_to(back[:1][None], sent.shape)


def base_powers_body(steps, smooth, base, top):
    square = smooth[...].T
    level = 0
    reach = 1
    while reach < steps:
        base[level] = square
        square = dot_nn(square, square)
        reach *= 2
        level += 1
    top[...] = square


def high_powers_body(count, outer_count, top, inner, outer):
    square = top[...]
    for dest, number in ((inner, count), (outer, outer_count)):
        level = 0
        reach = 1
        while reach < number:
            dest[level] = square
            square = dot_nn(square, square)
            reach *= 2
            level += 1


def lift_body(place, powers_ref, out):
    levels, n, _ = powers_ref.shape
    left = (1 << levels) - 1 - place[0]
    row = lax.broadcasted_iota(jnp.int32, (n, n), 0)
    column = lax.broadcasted_iota(jnp.int32, (n, n), 1)
    out[...] = jnp.where(row == column, 1.0, 0.0).astype(F32)
    for level in range(levels):
        @pl.when((left >> level) % 2 == 1)
        def _():
            out[...] = dot_nn(out[...], powers_ref[level])


def fold(rows, powers_ref):
    size = rows[0].shape[0]
    level = 0
    while len(rows) > 1:
        half = len(rows) // 2
        later = jnp.concatenate([rows[2 * i + 1] for i in range(half)], 0)
        moved = dot_nn(later, powers_ref[level])
        rows = [rows[2 * i] + moved[size * i : size * (i + 1)] for i in range(half)]
        level += 1
    return rows[0]


def backward_body(place, got, inner_powers, outer_powers, lifted, base_powers, top, base, out, totals):
    steps, n = base.shape
    outer_count = 1 << outer_powers.shape[0]
    inner_count = 1 << inner_powers.shape[0]
    here, group = place[0], place[1]

    def row(ref, index, inside):
        value = ref[pl.ds(jnp.where(inside, index, 0), 1), :]
        return jnp.broadcast_to(jnp.where(inside, value, jnp.zeros_like(value)), (PAD, n))

    blocks = []
    for k in range(inner_count):
        source = here + 1 + k
        mine = row(got, source * outer_count + group, source < inner_count)
        blocks.append(jnp.concatenate([got[k * outer_count : (k + 1) * outer_count, :], mine], 0))
    both = fold(blocks, inner_powers)
    totals[...] = both[:outer_count]
    after = both[outer_count:]
    blocks = []
    for k in range(outer_count):
        source = group + 1 + k
        blocks.append(row(totals, source, source < outer_count))
    boundary = after + dot_nn(fold(blocks, outer_powers), lifted[...])
    left = steps - lax.broadcasted_iota(jnp.int32, (steps, n), 0)
    back = jnp.broadcast_to(boundary[:1], (steps, n))
    factors = [base_powers[k] for k in range(base_powers.shape[0])] + [top[...]]
    for level, factor in enumerate(factors):
        back = jnp.where((left >> level) % 2 == 1, dot_nn(back, factor), back)
    out[...] = base[...] + back


def shards(jac, obs, gain_filter, gain_smooth, init_mean):
    steps, n, _ = jac.shape
    inner_count, outer_count = lax.axis_size("inner"), lax.axis_size("outer")
    counts = {"inner": inner_count, "outer": outer_count}
    inner, outer = lax.axis_index("inner"), lax.axis_index("outer")
    gain = gain_filter[None, :]

    def bit(index, k):
        return ((index >> k) % 2).astype(jnp.int32)[None]

    def exchange(total, axis, flip, beside):
        other = lax.ppermute(total, axis, [(i, i ^ flip) for i in range(counts[axis])])
        work = beside()
        return lax.optimization_barrier((other, work))

    with jax.named_scope("compose"):
        total, quarter, half, third = local_map(jac, obs, gain)

    def base_work():
        levels = steps.bit_length() - 1
        return kernel_call(
            functools.partial(base_powers_body, steps),
            [(levels, n, n), (n, n)],
            [VMEM],
            (gain_smooth,),
            "base_powers",
            flops=60 * n**3,
            size=20 * n * n,
        )

    with jax.named_scope("join_inner_0"):
        first, (base_powers, top) = exchange(total, "inner", 1, base_work)
        upper = bit(inner, 0)
        total = pair_call(total_body, upper, total, first, "total")

    with jax.named_scope("join_inner_1"):
        eye = jnp.concatenate([jnp.eye(n, dtype=F32), jnp.zeros((PAD, n), F32)], 0)
        second, before = exchange(total, "inner", 3, lambda: jnp.where(upper[0] == 1, first, eye))
        total = pair_call(total_body, bit(inner, 1), total, second, "total")

    with jax.named_scope("join_inner_2"):
        third_map, before = exchange(
            total, "inner", 4, lambda: pair_call(before_body, bit(inner, 1), before, second, "before")
        )
        total = pair_call(total_body, bit(inner, 2), total, third_map, "total")

    def three_work():
        three = kernel_call(
            join_body, (n + PAD, n), [VMEM, VMEM], (half, third), "join", flops=12 * n**3, size=12 * n * n
        )
        return three, pair_call(before_body, bit(inner, 2), before, third_map, "before")

    with jax.named_scope("join_inner_3"):
        other, (three, before) = exchange(total, "inner", 12, three_work)
        group_map = pair_call(total_body, bit(inner, 3), total, other, "total")
    with jax.named_scope("join_core"):
        twin, before = exchange(
            group_map, "outer", 1, lambda: pair_call(before_body, bit(inner, 3), before, other, "before")
        )
        total = pair_call(total_body, bit(outer, 0), group_map, twin, "total")
    with jax.named_scope("join_z"):
        other, before = exchange(
            total, "outer", 2, lambda: pair_call(before_body, bit(outer, 0), before, twin, "before")
        )
        total = pair_call(total_body, bit(outer, 1), total, other, "total")

    group = outer_count // 4
    super_here = outer // group
    x = jnp.broadcast_to(init_mean[None, :], (PAD, n))

    def mirror(source, dest):
        return [
            (source * group + z * 2 + c, dest * group + (group // 2 - 1 - z) * 2 + c)
            for z in range(group // 2)
            for c in range(2)
        ]

    with jax.named_scope("hop_0"):
        y = advance(x, total)
        arrived = lax.ppermute(y, "outer", mirror(0, 1))
        before = pair_call(before_body, bit(outer, 1), before, other, "before")
        arrived, before = lax.optimization_barrier((arrived, before))
        x = jnp.where(super_here == 1, arrived, x)
    with jax.named_scope("hop_1"):
        y = advance(x, total)
        near = lax.ppermute(y, "outer", mirror(1, 2))
        far = lax.ppermute(y, "outer", mirror(1, 3))
        skipped = lax.ppermute(total, "outer", mirror(2, 3))
        x = jnp.where(super_here == 2, near, x)
        x = jnp.where(super_here == 3, advance(far, skipped), x)
    with jax.named_scope("forward"):
        devices = inner_count * outer_count
        filt, base, sent = kernel_call(
            forward_body,
            [(steps, n), (steps, n), (devices, 1, n)],
            [VMEM] * 5 + [HBM] + [VMEM] * 3,
            (x, before, quarter, half, three, jac, obs, gain, base_powers),
            "forward",
            scratch=[
                pltpu.VMEM((steps, n), F32),
                pltpu.VMEM((2 * steps, n), F32),
                pltpu.VMEM((steps, n, n), F32),
                pltpu.SemaphoreType.DMA((steps,)),
            ],
            grant=52,
            flops=200 * steps * n * n,
            size=4 * steps * n * n,
        )
    def high_work():
        shapes = [(inner_count.bit_length() - 1, n, n), (outer_count.bit_length() - 1, n, n)]
        return kernel_call(
            functools.partial(high_powers_body, inner_count, outer_count),
            shapes,
            [VMEM],
            (top,),
            "high_powers",
            flops=90 * n**3,
            size=40 * n * n,
        )

    with jax.named_scope("offsets"):
        sent, top = lax.optimization_barrier((sent, top))
        got = lax.all_to_all(sent, ("inner", "outer"), 0, 0, tiled=True)
        inner_powers, outer_powers = high_work()
        lifted = kernel_call(
            lift_body,
            (n, n),
            [SMEM, VMEM],
            (inner.astype(jnp.int32)[None], inner_powers),
            "lift",
            flops=48 * n**3,
            size=20 * n * n,
        )
        got, lifted = lax.optimization_barrier((got.reshape(devices, n), lifted))
    with jax.named_scope("backward"):
        place = jnp.stack([inner, outer]).astype(jnp.int32)
        smoothed = kernel_call(
            backward_body,
            (steps, n),
            [SMEM] + [VMEM] * 7,
            (place, got, inner_powers, outer_powers, lifted, base_powers, top, base),
            "backward",
            scratch=[pltpu.VMEM((outer_count, n), F32)],
            flops=200 * n * n,
            size=24 * n * n,
        )
    return (filt, smoothed)


def solution(mesh):
    return jax.shard_map(
        shards,
        mesh=mesh,
        in_specs=(P(("outer", "inner"), None, None), P(("outer", "inner"), None), P(), P(), P()),
        out_specs=(P(("outer", "inner"), None), P(("outer", "inner"), None)),
        check_vma=False,
    )
```

time: 141 us -> 122 us (0.87)
  starting transfers between devices: 54.3 us -> 45.5 us
  Pallas kernels: 46.3 us -> 38.4 us
  waiting for transfers between devices: 34 us -> 31.5 us
    ppermute x9 -> x10, starting transfers between devices: 33.1 us -> 24.5 us  [the longest x6 16.7 us: exchange(): lax.ppermute(total, axis, [(i, i ^ flip) for i in range(counts[axis])])]
    pallas_call x20 -> x21, Pallas kernels: 46.3 us -> 38.4 us  [kernel_call(): pl.pallas_call(body, out_shape=shapes, in_specs=in_specs, out_specs=[VMEM...]
    ppermute x9 -> x10, waiting for transfers between devices: 27.5 us -> 22.3 us  [the longest x6 21.6 us: exchange(): lax.ppermute(total, axis, [(i, i ^ flip) for i in range(counts[axis])])]
    all_to_all x2 -> x1, waiting for transfers between devices: 6.5 us -> 9.19 us  [shards(): got = lax.all_to_all(sent, ('inner', 'outer'), 0, 0, tiled=True)]
    unnamed x20 -> x21, local copies, waits for them, and re-layouts: 3.62 us -> 5.02 us
    all_to_all x2 -> x1, starting transfers between devices: 21.2 us -> 21 us  [shards(): got = lax.all_to_all(sent, ('inner', 'outer'), 0, 0, tiled=True)]
  transfers between devices with their start and end apart: 11 -> 11, of which waited for: 11 -> 8; matrix products, arithmetic and copies ran while one was open for 0% -> 0% of each run, Pallas kernels for 6% -> 7%
where the time goes in v2:
time: 122 us
  starting transfers between devices  45.5 us (37%)
  Pallas kernels  38.4 us (31%)
  waiting for transfers between devices  31.5 us (26%)
  local copies, waits for them, and re-layouts  5.03 us (4%)
    pallas_call x21, Pallas kernels, kernel_call(): pl.pallas_call(body, out_shape=shapes, in_specs=in_specs, out_specs=[VMEM...  38.4 us
    ppermute x6, waiting for transfers between devices, exchange(): lax.ppermute(total, axis, [(i, i ^ flip) for i in range(counts[axis])])  21.6 us
    all_to_all x1, starting transfers between devices, shards(): got = lax.all_to_all(sent, ('inner', 'outer'), 0, 0, tiled=True)  21 us
    ppermute x6, starting transfers between devices, exchange(): lax.ppermute(total, axis, [(i, i ^ flip) for i in range(counts[axis])])  16.7 us
    all_to_all x1, waiting for transfers between devices, shards(): got = lax.all_to_all(sent, ('inner', 'outer'), 0, 0, tiled=True)  9.19 us
    ppermute x1, starting transfers between devices, shards(): arrived = lax.ppermute(y, 'outer', mirror(0, 1))  5.9 us
    unnamed x21, local copies, waits for them, and re-layouts  5.02 us
  transfers between devices with their start and end apart: 11, of which 8 were waited for; matrix products, arithmetic and copies ran while one was open for 0% of the time, Pallas kernels for 7%

profile of v2, /device:TPU:1, one launch (start us, length us, event | category | flops | bytes accessed | tf_op | source)
XLA Modules:
  0.0 121.5 jit_solution(5760544325723924233)
XLA Ops:
  2.0 9.2 %local_map.1 = (f32[264,256]{1,0:T(8,128)S(1)}, f32[264,256]{1,0:T(8,128)S(1)}, f32[264,256]{1,0:T(8,128)S(1)}, f32[264,256]{1,0:T(8,128)S(1)}) custom-call(f32[16,256,256]{2,1,0:T(8,128)} %jac_hbm.3, f32[16,256]{1,0:T(8,128)S(1)} %copy-done.4, f32[1,256]{1,0:T(1,128)S(1)} %bitcast.13), custom_call_target="tpu_custom_call" | custom-call | flops 3221225472 | bytes 4194304 | tf_op jit(solution)/shard_map/compose/local_map/pallas_call | solution.py:33
  11.2 2.2 %collective-permute-start = (f32[264,256]{1,0:T(8,128)S(1)}, f32[264,256]{1,0:T(8,128)S(1)}, u32[]{:S(2)}, u32[]{:S(2)}) collective-permute-start(f32[264,256]{1,0:T(8,128)S(1)} %get-tuple-element.33.own), channel_id=1, source_target_pairs={{0,16},{16,0},{32,48},{48,32},{64,80},{80,64},{96,112},{112,96},{1... | collective-permute-start | bytes 811016 | tf_op jit(solution)/shard_map/join_inner_0/ppermute | solution.py:292
  13.4 2.2 %base_powers.1 = (f32[4,256,256]{2,1,0:T(8,128)S(1)}, f32[256,256]{1,0:T(8,128)S(1)}) custom-call(f32[256,256]{1,0:T(8,128)S(1)} %copy-done.8), custom_call_target="tpu_custom_call" | custom-call | flops 1006632960 | bytes 1310720 | tf_op jit(solution)/shard_map/join_inner_0/base_powers/pallas_call | solution.py:33
  15.7 1.0 copy-done
  16.6 1.7 %collective-permute-done.other = f32[264,256]{1,0:T(8,128)S(1)} collective-permute-done((f32[264,256]{1,0:T(8,128)S(1)}, f32[264,256]{1,0:T(8,128)S(1)}, u32[]{:S(2)}, u32[]{:S(2)}) %collective-permute-start) | collective-permute-done | bytes 270368 | tf_op jit(solution)/shard_map/join_inner_0/ppermute | solution.py:292
  18.8 3.9 %collective-permute-start.1 = (f32[264,256]{1,0:T(8,128)S(1)}, f32[264,256]{1,0:T(8,128)S(1)}, u32[]{:S(2)}, u32[]{:S(2)}) collective-permute-start(f32[264,256]{1,0:T(8,128)S(1)} %total.6.own), channel_id=1, source_target_pairs={{0,48},{16,32},{32,16},{48,0},{64,112},{80,96},{96,80},{112,64},{1... | collective-permute-start | bytes 811016 | tf_op jit(solution)/shard_map/join_inner_1/ppermute | solution.py:292
  22.8 5.0 %collective-permute-done.1.other = f32[264,256]{1,0:T(8,128)S(1)} collective-permute-done((f32[264,256]{1,0:T(8,128)S(1)}, f32[264,256]{1,0:T(8,128)S(1)}, u32[]{:S(2)}, u32[]{:S(2)}) %collective-permute-start.1) | collective-permute-done | bytes 270368 | tf_op jit(solution)/shard_map/join_inner_1/ppermute | solution.py:292
  28.1 1.3 %collective-permute-start.2 = (f32[264,256]{1,0:T(8,128)S(1)}, f32[264,256]{1,0:T(8,128)S(1)}, u32[]{:S(2)}, u32[]{:S(2)}) collective-permute-start(f32[264,256]{1,0:T(8,128)S(1)} %total.7.own), channel_id=1, source_target_pairs={{0,64},{16,80},{32,96},{48,112},{64,0},{80,16},{96,32},{112,48},{1... | collective-permute-start | bytes 811016 | tf_op jit(solution)/shard_map/join_inner_2/ppermute | solution.py:292
  29.5 4.1 %collective-permute-done.2.other = f32[264,256]{1,0:T(8,128)S(1)} collective-permute-done((f32[264,256]{1,0:T(8,128)S(1)}, f32[264,256]{1,0:T(8,128)S(1)}, u32[]{:S(2)}, u32[]{:S(2)}) %collective-permute-start.2) | collective-permute-done | bytes 270368 | tf_op jit(solution)/shard_map/join_inner_2/ppermute | solution.py:292
  33.9 2.7 %collective-permute-start.3 = (f32[264,256]{1,0:T(8,128)S(1)}, f32[264,256]{1,0:T(8,128)S(1)}, u32[]{:S(2)}, u32[]{:S(2)}) collective-permute-start(f32[264,256]{1,0:T(8,128)S(1)} %total.8.own), channel_id=1, source_target_pairs={{0,192},{16,208},{32,224},{48,240},{64,128},{80,144},{96,160},{112... | collective-permute-start | bytes 811016 | tf_op jit(solution)/shard_map/join_inner_3/ppermute | solution.py:292
  37.1 3.6 %collective-permute-done.3.other = f32[264,256]{1,0:T(8,128)S(1)} collective-permute-done((f32[264,256]{1,0:T(8,128)S(1)}, f32[264,256]{1,0:T(8,128)S(1)}, u32[]{:S(2)}, u32[]{:S(2)}) %collective-permute-start.3) | collective-permute-done | bytes 270368 | tf_op jit(solution)/shard_map/join_inner_3/ppermute | solution.py:292
  41.1 4.8 %collective-permute-start.4 = (f32[264,256]{1,0:T(8,128)S(1)}, f32[264,256]{1,0:T(8,128)S(1)}, u32[]{:S(2)}, u32[]{:S(2)}) collective-permute-start(f32[264,256]{1,0:T(8,128)S(1)} %total.9.own), channel_id=1, source_target_pairs={{0,1},{1,0},{2,3},{3,2},{4,5},{5,4},{6,7},{7,6},{8,9},{9,8},{10,11... | collective-permute-start | bytes 811016 | tf_op jit(solution)/shard_map/join_core/ppermute | solution.py:292
  45.9 1.2 collective-permute-done.4.other
  47.5 1.7 %collective-permute-start.5 = (f32[264,256]{1,0:T(8,128)S(1)}, f32[264,256]{1,0:T(8,128)S(1)}, u32[]{:S(2)}, u32[]{:S(2)}) collective-permute-start(f32[264,256]{1,0:T(8,128)S(1)} %total.10.own), channel_id=1, source_target_pairs={{0,2},{1,3},{2,0},{3,1},{4,6},{5,7},{6,4},{7,5},{8,10},{9,11},{10,... | collective-permute-start | bytes 811016 | tf_op jit(solution)/shard_map/join_z/ppermute | solution.py:292
  49.6 6.0 %collective-permute-done.5.other = f32[264,256]{1,0:T(8,128)S(1)} collective-permute-done((f32[264,256]{1,0:T(8,128)S(1)}, f32[264,256]{1,0:T(8,128)S(1)}, u32[]{:S(2)}, u32[]{:S(2)}) %collective-permute-start.5) | collective-permute-done | bytes 270368 | tf_op jit(solution)/shard_map/join_z/ppermute | solution.py:292
  57.0 5.9 %collective-permute-start.6 = (f32[8,256]{1,0:T(8,128)S(1)}, f32[8,256]{1,0:T(8,128)S(1)}, u32[]{:S(2)}, u32[]{:S(2)}) collective-permute-start(f32[8,256]{1,0:T(8,128)S(1)} %advance.3), channel_id=1, source_target_pairs={{0,6},{1,7},{2,4},{3,5},{16,22},{17,23},{18,20},{19,21},{32,38},{3... | collective-permute-start | bytes 24584 | tf_op jit(solution)/shard_map/hop_0/ppermute | solution.py:360
  65.5 12.7 %forward.1 = (f32[16,256]{1,0:T(8,128)}, f32[16,256]{1,0:T(8,128)S(1)}, f32[256,1,256]{2,1,0:T(1,128)}) custom-call(f32[8,256]{1,0:T(8,128)S(1)} %select_select_fusion.x, f32[264,256]{1,0:T(8,128)S(1)} %before.9, f32[264,256]{1,0:T(8,128)S(1)} %get-tuple-element.51.quarter, f32[264,256]{1,0:T(8,128)S(1)} %get-tuple-element.40.earlier.half, ...), custom_call_target="tpu_custom_call" | custom-call | flops 209715200 | bytes 4194304 | tf_op jit(solution)/shard_map/forward/forward/pallas_call | solution.py:33
  78.2 21.0 %all-to-all-start = ((f32[256,1,256]{2,1,0:T(1,128)}), f32[256,1,256]{2,1,0:T(1,128)}, u32[]{:S(2)}, u32[]{:S(2)}) async-start(f32[256,1,256]{2,1,0:T(1,128)} %get-tuple-element.57), calls=%async_computation | async-start | bytes 524288 | tf_op jit(solution)/shard_map/offsets/all_to_all | solution.py:403
  99.3 3.5 %high_powers.1 = (f32[4,256,256]{2,1,0:T(8,128)S(1)}, f32[4,256,256]{2,1,0:T(8,128)S(1)}) custom-call(f32[256,256]{1,0:T(8,128)S(1)} %get-tuple-element.58.top), custom_call_target="tpu_custom_call" | custom-call | flops 1509949440 | bytes 2621440 | tf_op jit(solution)/shard_map/offsets/high_powers/pallas_call | solution.py:33
  102.8 1.6 %lift.1.lifted = f32[256,256]{1,0:T(8,128)S(1)} custom-call(s32[1]{0:T(128)} %bitcast.7.place, f32[4,256,256]{2,1,0:T(8,128)S(1)} %get-tuple-element.59.powers_ref.inner_powers), custom_call_target="tpu_custom_call" | custom-call | flops 805306368 | bytes 1310720 | tf_op jit(solution)/shard_map/offsets/lift/pallas_call | solution.py:33
  105.1 9.2 %all-to-all-done = f32[256,1,256]{2,1,0:T(1,128)} async-done(((f32[256,1,256]{2,1,0:T(1,128)}), f32[256,1,256]{2,1,0:T(1,128)}, u32[]{:S(2)}, u32[]{:S(2)}) %all-to-all-start) | async-done | bytes 262176 | tf_op jit(solution)/shard_map/offsets/all_to_all | solution.py:403
  114.2 1.0 copy.10
  115.2 0.9 copy-done.3
  116.2 5.4 %backward.1 = f32[16,256]{1,0:T(8,128)} custom-call(s32[2]{0:T(128)S(1)} %pad_add_fusion.place, f32[256,256]{1,0:T(8,128)S(1)} %bitcast.12, f32[4,256,256]{2,1,0:T(8,128)S(1)} %get-tuple-element.59.powers_ref.inner_powers, f32[4,256,256]{2,1,0:T(8,128)S(1)} %get-tuple-element.61.outer_powers, f32[256,256]{1,0:T(8,128)S(1)} %copy-done.3, ...), custom_call_target="tpu_custom_call" | custom-call | flops 13107200 | bytes 1572864 | tf_op jit(solution)/shard_map/backward/backward/pallas_call | solution.py:33
  (46 shorter events, 8.8 us)
Async XLA Ops:
  0.6 0.7 copy-start.4
  1.4 0.7 copy-start.6
  2.0 11.4 %copy-start.8 = (f32[256,256]{1,0:T(8,128)S(1)}, f32[256,256]{1,0:T(8,128)}, u32[]{:S(2)}) copy-start(f32[256,256]{1,0:T(8,128)} %smooth.1) | copy-start | bytes 786436
  11.2 7.2 %collective-permute-start = (f32[264,256]{1,0:T(8,128)S(1)}, f32[264,256]{1,0:T(8,128)S(1)}, u32[]{:S(2)}, u32[]{:S(2)}) collective-permute-start(f32[264,256]{1,0:T(8,128)S(1)} %get-tuple-element.33.own), channel_id=1, source_target_pairs={{0,16},{16,0},{32,48},{48,32},{64,80},{80,64},{96,112},{112,96},{1... | collective-permute-start | bytes 811016 | tf_op jit(solution)/shard_map/join_inner_0/ppermute | solution.py:292
  15.6 1.0 copy-start
  18.8 9.0 %collective-permute-start.1 = (f32[264,256]{1,0:T(8,128)S(1)}, f32[264,256]{1,0:T(8,128)S(1)}, u32[]{:S(2)}, u32[]{:S(2)}) collective-permute-start(f32[264,256]{1,0:T(8,128)S(1)} %total.6.own), channel_id=1, source_target_pairs={{0,48},{16,32},{32,16},{48,0},{64,112},{80,96},{96,80},{112,64},{1... | collective-permute-start | bytes 811016 | tf_op jit(solution)/shard_map/join_inner_1/ppermute | solution.py:292
  22.8 34.0 %copy-start.9 = (f32[256]{0:T(256)S(1)}, f32[256]{0:T(256)}, u32[]{:S(2)}) copy-start(f32[256]{0:T(256)} %param.9) | copy-start | bytes 3076
  28.1 5.4 %collective-permute-start.2 = (f32[264,256]{1,0:T(8,128)S(1)}, f32[264,256]{1,0:T(8,128)S(1)}, u32[]{:S(2)}, u32[]{:S(2)}) collective-permute-start(f32[264,256]{1,0:T(8,128)S(1)} %total.7.own), channel_id=1, source_target_pairs={{0,64},{16,80},{32,96},{48,112},{64,0},{80,16},{96,32},{112,48},{1... | collective-permute-start | bytes 811016 | tf_op jit(solution)/shard_map/join_inner_2/ppermute | solution.py:292
  29.4 36.0 %copy-start.5 = (f32[16,256]{1,0:T(8,128)S(1)}, f32[16,256]{1,0:T(8,128)}, u32[]{:S(2)}) copy-start(f32[16,256]{1,0:T(8,128)} %obs.1) | copy-start | bytes 49156
  29.4 36.0 %copy-start.7 = (f32[256]{0:T(256)S(1)}, f32[256]{0:T(256)}, u32[]{:S(2)}) copy-start(f32[256]{0:T(256)} %param.7) | copy-start | bytes 3076
  33.9 6.8 %collective-permute-start.3 = (f32[264,256]{1,0:T(8,128)S(1)}, f32[264,256]{1,0:T(8,128)S(1)}, u32[]{:S(2)}, u32[]{:S(2)}) collective-permute-start(f32[264,256]{1,0:T(8,128)S(1)} %total.8.own), channel_id=1, source_target_pairs={{0,192},{16,208},{32,224},{48,240},{64,128},{80,144},{96,160},{112... | collective-permute-start | bytes 811016 | tf_op jit(solution)/shard_map/join_inner_3/ppermute | solution.py:292
  41.1 6.0 %collective-permute-start.4 = (f32[264,256]{1,0:T(8,128)S(1)}, f32[264,256]{1,0:T(8,128)S(1)}, u32[]{:S(2)}, u32[]{:S(2)}) collective-permute-start(f32[264,256]{1,0:T(8,128)S(1)} %total.9.own), channel_id=1, source_target_pairs={{0,1},{1,0},{2,3},{3,2},{4,5},{5,4},{6,7},{7,6},{8,9},{9,8},{10,11... | collective-permute-start | bytes 811016 | tf_op jit(solution)/shard_map/join_core/ppermute | solution.py:292
  47.5 8.1 %collective-permute-start.5 = (f32[264,256]{1,0:T(8,128)S(1)}, f32[264,256]{1,0:T(8,128)S(1)}, u32[]{:S(2)}, u32[]{:S(2)}) collective-permute-start(f32[264,256]{1,0:T(8,128)S(1)} %total.10.own), channel_id=1, source_target_pairs={{0,2},{1,3},{2,0},{3,1},{4,6},{5,7},{6,4},{7,5},{8,10},{9,11},{10,... | collective-permute-start | bytes 811016 | tf_op jit(solution)/shard_map/join_z/ppermute | solution.py:292
  56.0 9.2 %collective-permute-start.8 = (f32[264,256]{1,0:T(8,128)S(1)}, f32[264,256]{1,0:T(8,128)S(1)}, u32[]{:S(2)}, u32[]{:S(2)}) collective-permute-start(f32[264,256]{1,0:T(8,128)S(1)} %total.11.refs_1_), channel_id=1, source_target_pairs={{8,14},{9,15},{10,12},{11,13},{24,30},{25,31},{26,28},{27,29},{40,... | collective-permute-start | bytes 811016 | tf_op jit(solution)/shard_map/hop_1/ppermute | solution.py:368
  57.0 6.7 %collective-permute-start.6 = (f32[8,256]{1,0:T(8,128)S(1)}, f32[8,256]{1,0:T(8,128)S(1)}, u32[]{:S(2)}, u32[]{:S(2)}) collective-permute-start(f32[8,256]{1,0:T(8,128)S(1)} %advance.3), channel_id=1, source_target_pairs={{0,6},{1,7},{2,4},{3,5},{16,22},{17,23},{18,20},{19,21},{32,38},{3... | collective-permute-start | bytes 24584 | tf_op jit(solution)/shard_map/hop_0/ppermute | solution.py:360
  63.9 1.3 %collective-permute-start.7 = (f32[8,256]{1,0:T(8,128)S(1)}, f32[8,256]{1,0:T(8,128)S(1)}, u32[]{:S(2)}, u32[]{:S(2)}) collective-permute-start(f32[8,256]{1,0:T(8,128)S(1)} %advance.4), channel_id=1, source_target_pairs={{4,14},{5,15},{6,12},{7,13},{20,30},{21,31},{22,28},{23,29},{36,46... | collective-permute-start | bytes 24584 | tf_op jit(solution)/shard_map/hop_1/ppermute | solution.py:367
  64.5 0.9 collective-permute-start.9
  78.2 36.0 %all-to-all-start = ((f32[256,1,256]{2,1,0:T(1,128)}), f32[256,1,256]{2,1,0:T(1,128)}, u32[]{:S(2)}, u32[]{:S(2)}) async-start(f32[256,1,256]{2,1,0:T(1,128)} %get-tuple-element.57), calls=%async_computation | async-start | bytes 524288 | tf_op jit(solution)/shard_map/offsets/all_to_all | solution.py:403
  99.3 16.0 %copy-start.1 = (f32[4,256,256]{2,1,0:T(8,128)S(1)}, f32[4,256,256]{2,1,0:T(8,128)}, u32[]{:S(2)}) copy-start(f32[4,256,256]{2,1,0:T(8,128)} %copy-done) | copy-start | bytes 3145732
  104.3 0.7 copy-start.2
  115.2 1.0 copy-start.3
